TPU v7x, 32 devices: a whole 2x2x4 slice. The times are simulated.
32 devices in a mesh: wide: 8 (over z, x), narrow: 4 (over y, core).
Axes of the slice: x: 2, y: 2, z: 4, core: 2. Of those that a mesh axis runs over, the one named last changes fastest.
Arguments:
- flow_field: bfloat16 [64, 64, 16, 512], P('wide', 'narrow'), may hold values from -48 to 48
- fluid_mask: int32 [64, 64, 16], P('wide', 'narrow'), may hold values 0 or 1
- conv_weight: float32 [27, 512], replicated, may hold values from -1 to 1
- latents: bfloat16 [1024, 512], replicated, may hold values from -6 to 6
- w_query1: bfloat16 [512, 512], replicated, may hold values from -0.25 to 0.25
- w_key1: bfloat16 [512, 512], replicated, may hold values from -0.25 to 0.25
- w_value1: bfloat16 [512, 512], replicated, may hold values from -0.25 to 0.25
- w_out1: bfloat16 [512, 512], replicated, may hold values from -0.25 to 0.25
- w_query2: bfloat16 [512, 512], replicated, may hold values from -0.25 to 0.25
- w_key2: bfloat16 [512, 512], replicated, may hold values from -0.25 to 0.25
- w_value2: bfloat16 [512, 512], replicated, may hold values from -0.25 to 0.25
- w_out2: bfloat16 [512, 512], replicated, may hold values from -0.25 to 0.25
Outputs:
- updated_field: float32 [64, 64, 16, 512], P('wide', 'narrow')
All inputs are finite; a program needn't handle non-finite values. No bound on the sum of `fluid_mask` on one device may be relied on, other than what follows from the above.
Results may differ from a plain program's by a relative error of at most 0.035.
The roundings to bfloat16 on the way count: a program that leaves them out, or rounds other values in their place, can miss the bound.
Values may be sent and summed in bfloat16 or wider, within the bound.
No kernel may reach another device: no remote copies, remote signals or barrier semaphores. Data moves between devices by JAX's collectives and lax.ppermute only.
A program may use at most 192 MiB of HBM per device.

v0:
```python
import math
import jax
import jax.numpy as jnp
from jax import lax
from jax.sharding import PartitionSpec as P

HEADS = 8


def padded_2(cells, sides, width):
    for axis, dim in sides:
        count = lax.axis_size(axis)
        ends = count - 1
        head = lax.slice_in_dim(cells, 0, width, axis=dim)
        tail = lax.slice_in_dim(cells, cells.shape[dim] - width, cells.shape[dim], axis=dim)
        cells = jnp.concatenate(
            [
                lax.ppermute(tail, axis, [(i, (i + 1) % count) for i in range(ends)]),
                cells,
                lax.ppermute(head, axis, [((i + 1) % count, i) for i in range(ends)]),
            ],
            axis=dim,
        )
    return cells


def head_block(matrix, head_index, head_size):
    return matrix[:, head_index * head_size : (head_index + 1) * head_size]


def pair_scores(queries, key_rows, head_size):
    factor = 1.8 / math.sqrt(head_size)
    return factor * lax.dot_general(
        queries, key_rows, (((1,), (1,)), ((), ())), preferred_element_type=jnp.float32
    )


def project(row_block, weight):
    return jnp.dot(row_block, weight, preferred_element_type=jnp.float32).astype(jnp.bfloat16)


def exact_dot(weights, values_block):
    return jnp.dot(
        weights, values_block, precision=lax.Precision.HIGHEST, preferred_element_type=jnp.float32
    )


def update_state(summed, totals, state_rows, w_out1, head_count):
    row_count, model_width = summed.shape
    shaped = summed.reshape(row_count, head_count, model_width // head_count) / totals[:, :, None]
    read_rows = shaped.reshape(row_count, model_width).astype(jnp.bfloat16)
    updated = state_rows.astype(jnp.float32) + jnp.dot(
        read_rows, w_out1, preferred_element_type=jnp.float32
    )
    return updated.astype(jnp.bfloat16)


def per_device(
    flow_field,
    fluid_mask,
    conv_weight,
    latents,
    w_query1,
    w_key1,
    w_value1,
    w_out1,
    w_query2,
    w_key2,
    w_value2,
    w_out2,
):
    size_x, size_y, size_z, model_width = flow_field.shape
    head_count = HEADS
    head_size = model_width // head_count
    latent_count = latents.shape[0]
    masked = flow_field * fluid_mask[:, :, :, None].astype(jnp.bfloat16)
    padded = padded_2(masked, (("wide", 0), ("narrow", 1)), 1)
    padded = jnp.pad(padded, ((0, 0), (0, 0), (1, 1), (0, 0)))
    stencil = masked.astype(jnp.float32)
    for offset_x in range(3):
        for offset_y in range(3):
            for offset_z in range(3):
                window = padded[
                    offset_x : offset_x + size_x,
                    offset_y : offset_y + size_y,
                    offset_z : offset_z + size_z,
                ]
                stencil = (
                    stencil
                    + window.astype(jnp.float32)
                    * conv_weight[9 * offset_x + 3 * offset_y + offset_z]
                )
    cell_count = size_x * size_y * size_z
    mixed_cells = stencil.astype(jnp.bfloat16).reshape(cell_count, model_width)
    flat_masked = masked.reshape(cell_count, model_width)
    keys1 = project(mixed_cells, w_key1)
    values1 = project(mixed_cells, w_value1)
    values_wide = values1.astype(jnp.float32)
    queries1 = project(latents, w_query1)
    device_count = lax.axis_size("wide") * lax.axis_size("narrow")
    sums_list = []
    totals_list = []
    tops_list = []
    for head_index in range(head_count):
        scores = pair_scores(
            head_block(queries1, head_index, head_size),
            head_block(keys1, head_index, head_size),
            head_size,
        )
        own_top = jnp.max(scores, axis=1, keepdims=True)
        weights = jnp.exp(scores - own_top)
        tops_list.append(own_top[:, 0])
        totals_list.append(jnp.sum(weights, axis=1))
        sums_list.append(exact_dot(weights, head_block(values_wide, head_index, head_size)))
    summed1 = jnp.concatenate(sums_list, axis=1)[None]
    totals1 = jnp.stack(totals_list, axis=1)[None]
    tops1 = jnp.stack(tops_list, axis=1)[None]
    part_sums, part_totals, part_tops = (
        lax.all_to_all(summed1, ("wide", "narrow"), split_axis=1, concat_axis=0, tiled=True),
        lax.all_to_all(totals1, ("wide", "narrow"), split_axis=1, concat_axis=0, tiled=True),
        lax.all_to_all(tops1, ("wide", "narrow"), split_axis=1, concat_axis=0, tiled=True),
    )
    row_count = latent_count // device_count
    largest = jnp.max(part_tops, axis=0, keepdims=True)
    factors = jnp.exp(part_tops - largest)
    totals = jnp.sum(factors * part_totals, axis=0)
    shaped = (
        part_sums.reshape(device_count, row_count, head_count, head_size) * factors[:, :, :, None]
    )
    summed = jnp.sum(shaped, axis=0).reshape(row_count, model_width)
    start = (
        lax.axis_index("wide") * lax.axis_size("narrow") + lax.axis_index("narrow")
    ) * row_count
    own_latents = lax.dynamic_slice_in_dim(latents, start, row_count, 0)
    own_state = update_state(summed, totals, own_latents, w_out1, head_count)
    latent_state = lax.all_gather(own_state, ("wide", "narrow"), axis=0, tiled=True)
    keys2 = project(latent_state, w_key2)
    values2 = project(latent_state, w_value2)
    queries2 = project(mixed_cells, w_query2)
    read_heads = []
    for head_index in range(head_count):
        scores = pair_scores(
            head_block(queries2, head_index, head_size),
            head_block(keys2, head_index, head_size),
            head_size,
        )
        top2 = jnp.max(scores, axis=1, keepdims=True)
        weights = jnp.exp(scores - top2)
        totals = jnp.sum(weights, axis=1, keepdims=True)
        summed = jnp.dot(
            weights.astype(jnp.bfloat16),
            head_block(values2, head_index, head_size),
            preferred_element_type=jnp.float32,
        )
        read_heads.append(summed / totals)
    read2 = jnp.concatenate(read_heads, axis=1).astype(jnp.bfloat16)
    result = flat_masked.astype(jnp.float32) + jnp.dot(
        read2, w_out2, preferred_element_type=jnp.float32
    )
    return result.reshape(size_x, size_y, size_z, model_width)


def solution(mesh):
    return jax.shard_map(
        per_device,
        mesh=mesh,
        in_specs=(
            P("wide", "narrow", None, None),
            P("wide", "narrow", None),
            P(),
            P(),
            P(),
            P(),
            P(),
            P(),
            P(),
            P(),
            P(),
            P(),
        ),
        out_specs=P("wide", "narrow", None, None),
        check_vma=False,
    )
```

profile of v0, /device:TPU:0, one launch (start us, length us, event | category | flops | bytes accessed | tf_op | source)
XLA Modules:
  0.0 399.7 jit_solution(2876258442550393296)
XLA Ops:
  9.5 4.9 %collective-permute-start = (bf16[1,16,16,512]{3,2,1,0:T(8,128)(2,1)S(1)}, bf16[1,16,16,512]{3,2,1,0:T(8,128)(2,1)S(1)}, u32[]{:S(2)}, u32[]{:S(2)}) collective-permute-start(bf16[1,16,16,512]{3,2,1,0:T(8,128)(2,1)S(1)} %get-tuple-element.11), channel_id=1, source_target_pairs={{0,4},{4,8},{8,12},{12,16},{16,20},{20,24},{24,28},{1,5},{5,9},{9,... | collective-permute-start | bytes 786440 | tf_op jit(solution)/shard_map/ppermute | solution.py:18
  16.6 9.0 %collective-permute-done = bf16[1,16,16,512]{3,2,1,0:T(8,128)(2,1)S(1)} collective-permute-done((bf16[1,16,16,512]{3,2,1,0:T(8,128)(2,1)S(1)}, bf16[1,16,16,512]{3,2,1,0:T(8,128)(2,1)S(1)}, u32[]{:S(2)}, u32[]{:S(2)}) %collective-permute-start) | collective-permute-done | bytes 262176 | tf_op jit(solution)/shard_map/ppermute | solution.py:18
  35.7 16.4 %add_convert_fusion = bf16[8,16,16,512]{3,2,1,0:T(8,128)(2,1)S(1)} fusion(bf16[8,16,16,512]{3,2,1,0:T(8,128)(2,1)S(1)} %broadcast_multiply_fusion, bf16[10,18,18,512]{3,2,1,0:T(8,128)(2,1)S(1)} %select_maximum_fusion, bf16[10,17,16,512]{3,2,1,0:T(8,128)(2,1)S(1)} %get-tuple-element.8, bf16[1,16,16,512]{3,2,1,0:T(8,128)(2,1)S(1)} %collective-permute-done.1, ...), kind=kLoop, calls=%fused_computation.91 | loop fusion | flops 88080384 | bytes 55105536 | tf_op jit(solution)/shard_map/convert_element_type | solution.py:94
  58.8 4.5 %multiply_reduce_fusion.12 = (f32[1024]{0:T(1024)S(1)}, f32[1024,2048]{1,0:T(8,128)}) fusion(bf16[2048,512]{0,1:T(8,128)(2,1)S(1)} %convolution_convert_fusion.1, bf16[1024,512]{0,1:T(8,128)(2,1)S(1)} %convolution_convert_fusion.5), kind=kOutput, calls=%fused_computation.31 | convolution fusion | flops 272628736 | bytes 8785920 | tf_op jit(solution)/shard_map/dot_general | solution.py:33
  63.3 4.5 %multiply_reduce_fusion.13 = (f32[1024]{0:T(1024)S(1)}, f32[1024,2048]{1,0:T(8,128)}) fusion(bf16[2048,512]{0,1:T(8,128)(2,1)S(1)} %convolution_convert_fusion.1, bf16[1024,512]{0,1:T(8,128)(2,1)S(1)} %convolution_convert_fusion.5), kind=kOutput, calls=%fused_computation.32 | convolution fusion | flops 272628736 | bytes 8785920 | tf_op jit(solution)/shard_map/dot_general | solution.py:33
  83.9 7.9 %fusion.149 = f32[1024,512]{0,1:T(8,128)S(1)} fusion(f32[1024,2048]{1,0:T(8,128)} %get-tuple-element.41, f32[1024]{0:T(1024)S(1)} %get-tuple-element.40, bf16[2048,512]{0,1:T(8,128)(2,1)} %convolution_convert_fusion), kind=kOutput, calls=%fused_computation.142 | convolution fusion | flops 1614807040 | bytes 8916992 | tf_op jit(solution)/shard_map/dot_general | solution.py:43
  96.2 8.1 %fusion.148 = f32[1024,512]{0,1:T(8,128)S(1)} fusion(f32[1024,512]{0,1:T(8,128)S(1)} %fusion.149, f32[1024,2048]{1,0:T(8,128)} %get-tuple-element.43, f32[1024]{0:T(1024)S(1)} %get-tuple-element.42, bf16[2048,512]{0,1:T(8,128)(2,1)} %convolution_convert_fusion), kind=kOutput, calls=%fused_computation.141 | convolution fusion | flops 1614807040 | bytes 8916992 | tf_op jit(solution)/shard_map/dot_general | solution.py:43
  108.7 8.1 %fusion.147 = f32[1024,512]{0,1:T(8,128)S(1)} fusion(f32[1024,512]{0,1:T(8,128)S(1)} %fusion.148, f32[1024,2048]{1,0:T(8,128)} %get-tuple-element.45, f32[1024]{0:T(1024)S(1)} %get-tuple-element.44, bf16[2048,512]{0,1:T(8,128)(2,1)} %convolution_convert_fusion), kind=kOutput, calls=%fused_computation.140 | convolution fusion | flops 1614807040 | bytes 8916992 | tf_op jit(solution)/shard_map/dot_general | solution.py:43
  121.1 8.3 %fusion.146 = f32[1024,512]{0,1:T(8,128)S(1)} fusion(f32[1024,512]{0,1:T(8,128)S(1)} %fusion.147, f32[1024,2048]{1,0:T(8,128)} %get-tuple-element.47, f32[1024]{0:T(1024)S(1)} %get-tuple-element.46, bf16[2048,512]{0,1:T(8,128)(2,1)} %convolution_convert_fusion), kind=kOutput, calls=%fused_computation.139 | convolution fusion | flops 1614807040 | bytes 8916992 | tf_op jit(solution)/shard_map/dot_general | solution.py:43
  131.4 6.5 %fusion.145 = f32[1024,512]{0,1:T(8,128)S(1)} fusion(f32[1024,512]{0,1:T(8,128)S(1)} %fusion.146, f32[1024,2048]{1,0:T(8,128)S(1)} %get-tuple-element.49, f32[1024]{0:T(1024)S(1)} %get-tuple-element.48, bf16[2048,512]{0,1:T(8,128)(2,1)} %convolution_convert_fusion), kind=kOutput, calls=%fused_computation.138 | convolution fusion | flops 1614807040 | bytes 8916992 | tf_op jit(solution)/shard_map/dot_general | solution.py:43
  140.2 6.5 %fusion.144 = f32[1024,512]{0,1:T(8,128)S(1)} fusion(f32[1024,512]{0,1:T(8,128)S(1)} %fusion.145, f32[1024,2048]{1,0:T(8,128)S(1)} %get-tuple-element.51, f32[1024]{0:T(1024)S(1)} %get-tuple-element.50, bf16[2048,512]{0,1:T(8,128)(2,1)} %convolution_convert_fusion), kind=kOutput, calls=%fused_computation.137 | convolution fusion | flops 1614807040 | bytes 8916992 | tf_op jit(solution)/shard_map/dot_general | solution.py:43
  154.3 9.5 %all-to-all-start.1 = ((f32[32,1,256]{2,1,0:T(1,128)}), f32[32,1,256]{2,1,0:T(1,128)S(1)}, u32[]{:S(2)}, u32[]{:S(2)}) async-start(f32[32,1,256]{2,1,0:T(1,128)} %reshape.112), calls=%async_computation.1 | async-start | bytes 65536 | tf_op jit(solution)/shard_map/all_to_all | solution.py:121
  163.8 8.1 %fusion.143 = f32[1024,512]{0,1:T(8,128)S(1)} fusion(f32[1024,512]{0,1:T(8,128)S(1)} %fusion.144, f32[1024,2048]{1,0:T(8,128)} %copy-done.3, f32[1024]{0:T(1024)S(1)} %get-tuple-element.52, bf16[2048,512]{0,1:T(8,128)(2,1)} %convolution_convert_fusion), kind=kOutput, calls=%fused_computation.136 | convolution fusion | flops 1614807040 | bytes 8916992 | tf_op jit(solution)/shard_map/dot_general | solution.py:43
  175.1 5.9 %all-to-all-start.2 = ((f32[32,1,256]{2,1,0:T(1,128)}), f32[32,1,256]{2,1,0:T(1,128)S(1)}, u32[]{:S(2)}, u32[]{:S(2)}) async-start(f32[32,1,256]{2,1,0:T(1,128)} %reshape.114), calls=%async_computation.2 | async-start | bytes 65536 | tf_op jit(solution)/shard_map/all_to_all | solution.py:120
  181.1 8.1 %fusion.142 = f32[1024,512]{0,1:T(8,128)S(1)} fusion(f32[1024,512]{0,1:T(8,128)S(1)} %fusion.143, f32[1024,2048]{1,0:T(8,128)} %copy-done.2, f32[1024]{0:T(1024)S(1)} %get-tuple-element.54, bf16[2048,512]{0,1:T(8,128)(2,1)} %convolution_convert_fusion), kind=kOutput, calls=%fused_computation.135 | convolution fusion | flops 1614807040 | bytes 8916992 | tf_op jit(solution)/shard_map/dot_general | solution.py:43
  192.9 6.0 %all-to-all-start = ((f32[1,1024,512]{2,0,1:T(1,128)}), f32[1,1024,512]{2,0,1:T(1,128)}, u32[]{:S(2)}, u32[]{:S(2)}) async-start(f32[1,1024,512]{2,0,1:T(1,128)} %copy.23), calls=%async_computation | async-start | bytes 4194304 | tf_op jit(solution)/shard_map/all_to_all | solution.py:119
  209.5 38.1 %all-to-all-done = f32[1,1024,512]{2,0,1:T(1,128)} async-done(((f32[1,1024,512]{2,0,1:T(1,128)}), f32[1,1024,512]{2,0,1:T(1,128)}, u32[]{:S(2)}, u32[]{:S(2)}) %all-to-all-start) | async-done | bytes 2097184 | tf_op jit(solution)/shard_map/all_to_all | solution.py:119
  254.4 50.3 %all-gather.2.cloned.1.call-done = bf16[1024,512]{1,0:T(8,128)(2,1)} async-done(((bf16[32,512]{1,0:T(8,128)(2,1)}), bf16[1024,512]{1,0:T(8,128)(2,1)}) %all-gather.2.cloned.1.call-update) | async-done | bytes 1048592 | tf_op jit(solution)/shard_map/all_gather | solution.py:136
  310.6 4.5 %multiply_reduce_fusion.3 = (f32[2048]{0:T(1024)S(1)}, f32[2048,1024]{0,1:T(8,128)}) fusion(bf16[1024,512]{0,1:T(8,128)(2,1)S(1)} %convolution_convert_fusion.4, bf16[2048,512]{0,1:T(8,128)(2,1)S(1)} %convolution_convert_fusion.2), kind=kOutput, calls=%fused_computation.22 | convolution fusion | flops 272627712 | bytes 8790016 | tf_op jit(solution)/shard_map/dot_general | solution.py:33
  315.1 4.5 %multiply_reduce_fusion.4 = (f32[2048]{0:T(1024)S(1)}, f32[2048,1024]{0,1:T(8,128)}) fusion(bf16[1024,512]{0,1:T(8,128)(2,1)S(1)} %convolution_convert_fusion.4, bf16[2048,512]{0,1:T(8,128)(2,1)S(1)} %convolution_convert_fusion.2), kind=kOutput, calls=%fused_computation.23 | convolution fusion | flops 272627712 | bytes 8790016 | tf_op jit(solution)/shard_map/dot_general | solution.py:33
  319.6 4.5 %multiply_reduce_fusion.5 = (f32[2048]{0:T(1024)S(1)}, f32[2048,1024]{0,1:T(8,128)}) fusion(bf16[1024,512]{0,1:T(8,128)(2,1)S(1)} %convolution_convert_fusion.4, bf16[2048,512]{0,1:T(8,128)(2,1)S(1)} %convolution_convert_fusion.2), kind=kOutput, calls=%fused_computation.24 | convolution fusion | flops 272627712 | bytes 8790016 | tf_op jit(solution)/shard_map/dot_general | solution.py:33
  324.2 4.5 %multiply_reduce_fusion.6 = (f32[2048]{0:T(1024)S(1)}, f32[2048,1024]{0,1:T(8,128)}) fusion(bf16[1024,512]{0,1:T(8,128)(2,1)S(1)} %convolution_convert_fusion.4, bf16[2048,512]{0,1:T(8,128)(2,1)S(1)} %convolution_convert_fusion.2), kind=kOutput, calls=%fused_computation.25 | convolution fusion | flops 272627712 | bytes 8790016 | tf_op jit(solution)/shard_map/dot_general | solution.py:33
  328.7 5.0 %multiply_reduce_fusion.7 = (f32[2048]{0:T(1024)S(1)}, f32[2048,1024]{0,1:T(8,128)}) fusion(bf16[1024,512]{0,1:T(8,128)(2,1)S(1)} %convolution_convert_fusion.4, bf16[2048,512]{0,1:T(8,128)(2,1)S(1)} %convolution_convert_fusion.2), kind=kOutput, calls=%fused_computation.26 | convolution fusion | flops 272627712 | bytes 8790016 | tf_op jit(solution)/shard_map/dot_general | solution.py:33
  337.9 4.8 %fusion.25 = f32[2048]{0:T(1024)S(1)} fusion(f32[2048,1024]{0,1:T(8,128)} %get-tuple-element.65, f32[2048]{0:T(1024)S(1)} %get-tuple-element.64), kind=kLoop, calls=%fused_computation.59 | loop fusion | flops 6289408 | bytes 8404992 | tf_op jit(solution)/shard_map/reduce_sum | solution.py:149
  342.7 4.8 %fusion.23 = f32[2048]{0:T(1024)S(1)} fusion(f32[2048,1024]{0,1:T(8,128)} %get-tuple-element.63, f32[2048]{0:T(1024)S(1)} %get-tuple-element.62), kind=kLoop, calls=%fused_computation.57 | loop fusion | flops 6289408 | bytes 8404992 | tf_op jit(solution)/shard_map/reduce_sum | solution.py:149
  347.4 4.8 %fusion.21 = f32[2048]{0:T(1024)S(1)} fusion(f32[2048,1024]{0,1:T(8,128)} %get-tuple-element.61, f32[2048]{0:T(1024)S(1)} %get-tuple-element.60), kind=kLoop, calls=%fused_computation.55 | loop fusion | flops 6289408 | bytes 8404992 | tf_op jit(solution)/shard_map/reduce_sum | solution.py:149
  352.2 4.8 %fusion.19 = f32[2048]{0:T(1024)S(1)} fusion(f32[2048,1024]{0,1:T(8,128)} %get-tuple-element.59, f32[2048]{0:T(1024)S(1)} %get-tuple-element.58), kind=kLoop, calls=%fused_computation.53 | loop fusion | flops 6289408 | bytes 8404992 | tf_op jit(solution)/shard_map/reduce_sum | solution.py:149
  357.0 5.1 %fusion.17 = f32[2048]{0:T(1024)S(1)} fusion(f32[2048,1024]{0,1:T(8,128)} %get-tuple-element.57, f32[2048]{0:T(1024)S(1)} %get-tuple-element.56), kind=kLoop, calls=%fused_computation.51 | loop fusion | flops 6289408 | bytes 8404992 | tf_op jit(solution)/shard_map/reduce_sum | solution.py:149
  362.9 4.9 %fusion.76 = bf16[2048,512]{0,1:T(8,128)(2,1)S(1)} fusion(f32[2048,1024]{0,1:T(8,128)} %get-tuple-element.57, f32[2048]{0:T(1024)S(1)} %get-tuple-element.56, f32[2048]{0:T(1024)S(1)} %fusion.17, bf16[1024,512]{0,1:T(8,128)(2,1)S(1)} %convolution_convert_fusion.3), kind=kOutput, calls=%fused_computation.107 | convolution fusion | flops 274989056 | bytes 8798208 | tf_op jit(solution)/shard_map/dot_general | solution.py:150
  367.8 4.9 %fusion.85 = bf16[2048,512]{0,1:T(8,128)(2,1)S(1)} fusion(bf16[2048,512]{0,1:T(8,128)(2,1)S(1)} %fusion.76, f32[2048,1024]{0,1:T(8,128)} %get-tuple-element.59, f32[2048]{0:T(1024)S(1)} %get-tuple-element.58, f32[2048]{0:T(1024)S(1)} %fusion.19, bf16[1024,512]{0,1:T(8,128)(2,1)S(1)} %convolution_convert_fusion.3), kind=kOutput, calls=%fused_computation.110 | convolution fusion | flops 274989056 | bytes 8798208 | tf_op jit(solution)/shard_map/dot_general | solution.py:150
  372.8 5.1 %fusion.94 = bf16[2048,512]{0,1:T(8,128)(2,1)S(1)} fusion(bf16[2048,512]{0,1:T(8,128)(2,1)S(1)} %fusion.85, f32[2048,1024]{0,1:T(8,128)} %get-tuple-element.61, f32[2048]{0:T(1024)S(1)} %get-tuple-element.60, f32[2048]{0:T(1024)S(1)} %fusion.21, bf16[1024,512]{0,1:T(8,128)(2,1)S(1)} %convolution_convert_fusion.3), kind=kOutput, calls=%fused_computation.113 | convolution fusion | flops 274989056 | bytes 8798208 | tf_op jit(solution)/shard_map/dot_general | solution.py:150
  377.8 5.1 %fusion.103 = bf16[2048,512]{0,1:T(8,128)(2,1)S(1)} fusion(bf16[2048,512]{0,1:T(8,128)(2,1)S(1)} %fusion.94, f32[2048,1024]{0,1:T(8,128)} %get-tuple-element.63, f32[2048]{0:T(1024)S(1)} %get-tuple-element.62, f32[2048]{0:T(1024)S(1)} %fusion.23, bf16[1024,512]{0,1:T(8,128)(2,1)S(1)} %convolution_convert_fusion.3), kind=kOutput, calls=%fused_computation.116 | convolution fusion | flops 274989056 | bytes 8798208 | tf_op jit(solution)/shard_map/dot_general | solution.py:150
  (116 shorter events, 107.6 us)
Async XLA Ops:
  6.5 45.5 %copy-start = (bf16[512,512]{1,0:T(8,128)(2,1)S(1)}, bf16[512,512]{1,0:T(8,128)(2,1)}, u32[]{:S(2)}) copy-start(bf16[512,512]{1,0:T(8,128)(2,1)} %param.17) | copy-start | bytes 1572868
  6.5 9.2 %copy-start.9 = (f32[27,512]{1,0:T(8,128)S(1)}, f32[27,512]{1,0:T(8,128)}, u32[]{:S(2)}) copy-start(f32[27,512]{1,0:T(8,128)} %param.14) | copy-start | bytes 165892
  6.5 9.2 %copy-start.10 = (bf16[1024,512]{1,0:T(8,128)(2,1)S(1)}, bf16[1024,512]{1,0:T(8,128)(2,1)}, u32[]{:S(2)}) copy-start(bf16[1024,512]{1,0:T(8,128)(2,1)} %param.15) | copy-start | bytes 3145732
  6.5 9.2 %copy-start.12 = (bf16[512,512]{1,0:T(8,128)(2,1)S(1)}, bf16[512,512]{1,0:T(8,128)(2,1)}, u32[]{:S(2)}) copy-start(bf16[512,512]{1,0:T(8,128)(2,1)} %param.16) | copy-start | bytes 1572868
  9.5 26.2 %copy-start.4 = (bf16[8,16,16,512]{3,2,1,0:T(8,128)(2,1)}, bf16[8,16,16,512]{3,2,1,0:T(8,128)(2,1)S(1)}, u32[]{:S(2)}) copy-start(bf16[8,16,16,512]{3,2,1,0:T(8,128)(2,1)S(1)} %broadcast_multiply_fusion) | copy-start | bytes 6291460
  9.5 16.0 %collective-permute-start = (bf16[1,16,16,512]{3,2,1,0:T(8,128)(2,1)S(1)}, bf16[1,16,16,512]{3,2,1,0:T(8,128)(2,1)S(1)}, u32[]{:S(2)}, u32[]{:S(2)}) collective-permute-start(bf16[1,16,16,512]{3,2,1,0:T(8,128)(2,1)S(1)} %get-tuple-element.11), channel_id=1, source_target_pairs={{0,4},{4,8},{8,12},{12,16},{16,20},{20,24},{24,28},{1,5},{5,9},{9,... | collective-permute-start | bytes 786440 | tf_op jit(solution)/shard_map/ppermute | solution.py:18
  14.4 11.2 %collective-permute-start.1 = (bf16[1,16,16,512]{3,2,1,0:T(8,128)(2,1)S(1)}, bf16[1,16,16,512]{3,2,1,0:T(8,128)(2,1)S(1)}, u32[]{:S(2)}, u32[]{:S(2)}) collective-permute-start(bf16[1,16,16,512]{3,2,1,0:T(8,128)(2,1)S(1)} %get-tuple-element.12), channel_id=1, source_target_pairs={{4,0},{8,4},{12,8},{16,12},{20,16},{24,20},{28,24},{5,1},{9,5},{13... | collective-permute-start | bytes 786440 | tf_op jit(solution)/shard_map/ppermute | solution.py:20
  25.6 2.6 collective-permute-start.2
  26.9 5.0 %collective-permute-start.3 = (bf16[10,1,16,512]{3,2,1,0:T(8,128)(2,1)S(1)}, bf16[10,1,16,512]{3,2,1,0:T(8,128)(2,1)S(1)}, u32[]{:S(2)}, u32[]{:S(2)}) collective-permute-start(bf16[10,1,16,512]{3,2,1,0:T(8,128)(2,1)S(1)} %get-tuple-element.10), channel_id=1, source_target_pairs={{1,0},{2,1},{3,2},{5,4},{6,5},{7,6},{9,8},{10,9},{11,10},{13,12},{... | collective-permute-start | bytes 491528 | tf_op jit(solution)/shard_map/ppermute | solution.py:20
  52.1 24.7 %copy-start.6 = (bf16[8,16,16,512]{3,2,1,0:T(8,128)(2,1)}, bf16[8,16,16,512]{3,2,1,0:T(8,128)(2,1)S(1)}, u32[]{:S(2)}) copy-start(bf16[8,16,16,512]{3,2,1,0:T(8,128)(2,1)S(1)} %add_convert_fusion) | copy-start | bytes 6291460
  54.7 92.0 %copy-start.2 = (f32[1024,2048]{1,0:T(8,128)}, f32[1024,2048]{1,0:T(8,128)S(1)}, u32[]{:S(2)}) copy-start(f32[1024,2048]{1,0:T(8,128)S(1)} %get-tuple-element.55) | copy-start | bytes 25165828
  56.1 92.5 %copy-start.3 = (f32[1024,2048]{1,0:T(8,128)}, f32[1024,2048]{1,0:T(8,128)S(1)}, u32[]{:S(2)}) copy-start(f32[1024,2048]{1,0:T(8,128)S(1)} %get-tuple-element.53) | copy-start | bytes 25165828
  72.3 4.5 %copy-start.13 = (bf16[512,512]{1,0:T(8,128)(2,1)S(1)}, bf16[512,512]{1,0:T(8,128)(2,1)}, u32[]{:S(2)}) copy-start(bf16[512,512]{1,0:T(8,128)(2,1)} %param.18) | copy-start | bytes 1572868
  154.3 20.8 %all-to-all-start.1 = ((f32[32,1,256]{2,1,0:T(1,128)}), f32[32,1,256]{2,1,0:T(1,128)S(1)}, u32[]{:S(2)}, u32[]{:S(2)}) async-start(f32[32,1,256]{2,1,0:T(1,128)} %reshape.112), calls=%async_computation.1 | async-start | bytes 65536 | tf_op jit(solution)/shard_map/all_to_all | solution.py:121
  175.1 17.8 %all-to-all-start.2 = ((f32[32,1,256]{2,1,0:T(1,128)}), f32[32,1,256]{2,1,0:T(1,128)S(1)}, u32[]{:S(2)}, u32[]{:S(2)}) async-start(f32[32,1,256]{2,1,0:T(1,128)} %reshape.114), calls=%async_computation.2 | async-start | bytes 65536 | tf_op jit(solution)/shard_map/all_to_all | solution.py:120
  192.9 54.7 %all-to-all-start = ((f32[1,1024,512]{2,0,1:T(1,128)}), f32[1,1024,512]{2,0,1:T(1,128)}, u32[]{:S(2)}, u32[]{:S(2)}) async-start(f32[1,1024,512]{2,0,1:T(1,128)} %copy.23), calls=%async_computation | async-start | bytes 4194304 | tf_op jit(solution)/shard_map/all_to_all | solution.py:119
  198.9 105.8 %all-gather.2.cloned.1.call-start = ((), (), s32[]{:S(2)}) async-start(), calls=%async_computation.3 | async-start | bytes 1081344 | tf_op jit(solution)/shard_map/all_gather | solution.py:136
  209.4 40.4 %copy-start.8 = (bf16[512,512]{1,0:T(8,128)(2,1)S(1)}, bf16[512,512]{1,0:T(8,128)(2,1)}, u32[]{:S(2)}) copy-start(bf16[512,512]{1,0:T(8,128)(2,1)} %param.19) | copy-start | bytes 1572868
  209.5 42.0 %copy-start.14 = (bf16[512,512]{1,0:T(8,128)(2,1)S(1)}, bf16[512,512]{1,0:T(8,128)(2,1)}, u32[]{:S(2)}) copy-start(bf16[512,512]{1,0:T(8,128)(2,1)} %param.20) | copy-start | bytes 1572868
  251.4 53.2 %copy-start.15 = (bf16[512,512]{1,0:T(8,128)(2,1)S(1)}, bf16[512,512]{1,0:T(8,128)(2,1)}, u32[]{:S(2)}) copy-start(bf16[512,512]{1,0:T(8,128)(2,1)} %param.21) | copy-start | bytes 1572868
  357.0 5.1 %copy-start.11 = (bf16[1024,512]{1,0:T(8,128)(2,1)S(1)}, bf16[1024,512]{1,0:T(8,128)(2,1)}, u32[]{:S(2)}) copy-start(bf16[1024,512]{1,0:T(8,128)(2,1)} %all-gather.2.cloned.1.call-done) | copy-start | bytes 3145732
  357.0 5.1 %copy-start.16 = (bf16[512,512]{1,0:T(8,128)(2,1)S(1)}, bf16[512,512]{1,0:T(8,128)(2,1)}, u32[]{:S(2)}) copy-start(bf16[512,512]{1,0:T(8,128)(2,1)} %param.22) | copy-start | bytes 1572868
  372.7 10.2 %slice-start = ((s8[8388608]{0:T(1024)(128)(4,1)}), s8[4194304]{0:T(1024)(128)(4,1)S(1)}, s32[]{:S(2)}) async-start(s8[8388608]{0:T(1024)(128)(4,1)} %bitcast.74), calls=%async_computation.4 | async-start | bytes 8388608
  377.8 5.1 %slice-start.1 = ((s8[8388608]{0:T(1024)(128)(4,1)}), s8[4194304]{0:T(1024)(128)(4,1)S(1)}, s32[]{:S(2)}) async-start(s8[8388608]{0:T(1024)(128)(4,1)} %bitcast.74), calls=%async_computation.5 | async-start | bytes 8388608
  387.6 1.6 copy-start.5
  387.6 1.7 copy-start.7
  387.6 5.0 %copy-start.1 = (bf16[512,512]{1,0:T(8,128)(2,1)S(1)}, bf16[512,512]{1,0:T(8,128)(2,1)}, u32[]{:S(2)}) copy-start(bf16[512,512]{1,0:T(8,128)(2,1)} %param.17) | copy-start | bytes 1572868
Sparse Core Ops, SparseCore 0:
  251.5 53.0 all-gather.1
where the time goes:
time: 405 us; the launch traced here: 400 us
  matrix products  154 us (38%)
  waiting for transfers between devices  101 us (25%)
  other arithmetic  82.8 us (20%)
  starting transfers between devices  30.2 us (7%)
  local copies, waits for them, and re-layouts  17.8 us (4%)
  between operations  14.2 us (4%)
    dot_general x8, matrix products, exact_dot(): jnp.dot(weights, values_block, precision=lax.Precision.HIGHEST, preferred...  61.6 us
    dot_general x16, matrix products, pair_scores(): lax.dot_general(queries, key_rows, (((1,), (1,)), ((), ())), preferred_el...  50.3 us
    all_gather x1, waiting for transfers between devices, per_device(): lax.all_gather(own_state, ('wide', 'narrow'), axis=0, tiled=True)  50.3 us
    all_to_all x1, waiting for transfers between devices, per_device(): lax.all_to_all(summed1, ('wide', 'narrow'), split_axis=1, concat_axis=0,...  38.1 us
    reduce_sum x8, other arithmetic, per_device(): totals = jnp.sum(weights, axis=1, keepdims=True)  28.4 us
    dot_general x8, matrix products, per_device(): jnp.dot(weights.astype(jnp.bfloat16), head_block(values2, head_index, hea...  26.2 us
    reduce_sum x8, other arithmetic, per_device(): totals_list.append(jnp.sum(weights, axis=1))  25.6 us
    convert_element_type x1, other arithmetic, per_device(): mixed_cells = stencil.astype(jnp.bfloat16).reshape(cell_count, model_width)  16.4 us
  transfers between devices with their start and end apart: 8, of which 4 were waited for; matrix products, arithmetic and copies ran while one was open for 9% of the time, Pallas kernels for 0%

commit v1 on v0

--- a/solution.py
+++ b/solution.py
@@ -5,6 +5,13 @@
 from jax.sharding import PartitionSpec as P
 
 HEADS = 8
+
+
+def swap_blocks(x, axis, split, join):
+    size = lax.axis_size(axis)
+    tiles = jnp.stack(jnp.split(x, size, axis=split), axis=0)
+    tiles = lax.all_to_all(tiles, axis, split_axis=0, concat_axis=0)
+    return jnp.concatenate(tiles, axis=join)
 
 
 def padded_2(cells, sides, width):
@@ -116,7 +123,7 @@
     totals1 = jnp.stack(totals_list, axis=1)[None]
     tops1 = jnp.stack(tops_list, axis=1)[None]
     part_sums, part_totals, part_tops = (
-        lax.all_to_all(summed1, ("wide", "narrow"), split_axis=1, concat_axis=0, tiled=True),
+        swap_blocks(summed1, ("wide", "narrow"), 1, 0),
         lax.all_to_all(totals1, ("wide", "narrow"), split_axis=1, concat_axis=0, tiled=True),
         lax.all_to_all(tops1, ("wide", "narrow"), split_axis=1, concat_axis=0, tiled=True),
     )

time: 405 us -> 460 us (1.14)
  local copies, waits for them, and re-layouts: 17.8 us -> 73.4 us
  matrix products: 154 us -> 146 us
  waiting for transfers between devices: 101 us -> 107 us
    another operation x0 -> x35, local copies, waits for them, and re-layouts: none -> 34.9 us  [swap_blocks(): tiles = jnp.stack(jnp.split(x, size, axis=split), axis=0)]
    unnamed x44 -> x76, local copies, waits for them, and re-layouts: 5.99 us -> 30.5 us
    dot_general x8, matrix products: 61.6 us -> 54.4 us  [exact_dot(): jnp.dot(weights, values_block, precision=lax.Precision.HIGHEST, preferred...]
    all_to_all x1, waiting for transfers between devices: 0.01 us -> 6.62 us  [per_device(): lax.all_to_all(totals1, ('wide', 'narrow'), split_axis=1, concat_axis=0,...]
  transfers between devices with their start and end apart: 8 -> 8, of which waited for: 4 -> 5; matrix products, arithmetic and copies ran while one was open for 9% -> 16% of each run, Pallas kernels for 0% -> 0%
where the time goes in v1:
time: 460 us; the launch traced here: 454 us
  matrix products  146 us (32%)
  waiting for transfers between devices  107 us (23%)
  other arithmetic  85.7 us (19%)
  local copies, waits for them, and re-layouts  73.4 us (16%)
  starting transfers between devices  27.9 us (6%)
  between operations  14.2 us (3%)
    dot_general x8, matrix products, exact_dot(): jnp.dot(weights, values_block, precision=lax.Precision.HIGHEST, preferred...  54.4 us
    all_gather x1, waiting for transfers between devices, per_device(): lax.all_gather(own_state, ('wide', 'narrow'), axis=0, tiled=True)  50.1 us
    dot_general x16, matrix products, pair_scores(): lax.dot_general(queries, key_rows, (((1,), (1,)), ((), ())), preferred_el...  50.1 us
    all_to_all x1, waiting for transfers between devices, swap_blocks(): tiles = lax.all_to_all(tiles, axis, split_axis=0, concat_axis=0)  37.2 us
    another operation x35, local copies, waits for them, and re-layouts, swap_blocks(): tiles = jnp.stack(jnp.split(x, size, axis=split), axis=0)  34.9 us
    unnamed x76, local copies, waits for them, and re-layouts  30.5 us
    reduce_sum x8, other arithmetic, per_device(): totals = jnp.sum(weights, axis=1, keepdims=True)  28.5 us
    dot_general x8, matrix products, per_device(): jnp.dot(weights.astype(jnp.bfloat16), head_block(values2, head_index, hea...  26.2 us
  transfers between devices with their start and end apart: 8, of which 5 were waited for; matrix products, arithmetic and copies ran while one was open for 16% of the time, Pallas kernels for 0%

profile of v1, /device:TPU:0, one launch (start us, length us, event | category | flops | bytes accessed | tf_op | source)
XLA Modules:
  0.0 454.2 jit_solution(10307164598530181682)
XLA Ops:
  9.5 4.9 %collective-permute-start = (bf16[1,16,16,512]{3,2,1,0:T(8,128)(2,1)S(1)}, bf16[1,16,16,512]{3,2,1,0:T(8,128)(2,1)S(1)}, u32[]{:S(2)}, u32[]{:S(2)}) collective-permute-start(bf16[1,16,16,512]{3,2,1,0:T(8,128)(2,1)S(1)} %get-tuple-element.43), channel_id=1, source_target_pairs={{0,4},{4,8},{8,12},{12,16},{16,20},{20,24},{24,28},{1,5},{5,9},{9,... | collective-permute-start | bytes 786440 | tf_op jit(solution)/shard_map/ppermute | solution.py:25
  16.6 9.0 %collective-permute-done = bf16[1,16,16,512]{3,2,1,0:T(8,128)(2,1)S(1)} collective-permute-done((bf16[1,16,16,512]{3,2,1,0:T(8,128)(2,1)S(1)}, bf16[1,16,16,512]{3,2,1,0:T(8,128)(2,1)S(1)}, u32[]{:S(2)}, u32[]{:S(2)}) %collective-permute-start) | collective-permute-done | bytes 262176 | tf_op jit(solution)/shard_map/ppermute | solution.py:25
  35.7 16.4 %add_convert_fusion = bf16[8,16,16,512]{3,2,1,0:T(8,128)(2,1)S(1)} fusion(bf16[8,16,16,512]{3,2,1,0:T(8,128)(2,1)S(1)} %broadcast_multiply_fusion, bf16[10,18,18,512]{3,2,1,0:T(8,128)(2,1)S(1)} %select_maximum_fusion, bf16[10,17,16,512]{3,2,1,0:T(8,128)(2,1)S(1)} %get-tuple-element.8, bf16[1,16,16,512]{3,2,1,0:T(8,128)(2,1)S(1)} %collective-permute-done.1, ...), kind=kLoop, calls=%fused_computation.91 | loop fusion | flops 88080384 | bytes 55105536 | tf_op jit(solution)/shard_map/convert_element_type | solution.py:101
  58.8 4.5 multiply_reduce_fusion.12
  67.8 4.5 multiply_reduce_fusion.14
  84.1 7.8 %fusion.149 = f32[1024,512]{0,1:T(8,128)S(1)} fusion(f32[1024,2048]{1,0:T(8,128)} %get-tuple-element.73, f32[1024]{0:T(1024)S(1)} %get-tuple-element.72, bf16[2048,512]{0,1:T(8,128)(2,1)S(1)} %copy-done.5), kind=kOutput, calls=%fused_computation.142 | convolution fusion | flops 1614807040 | bytes 8916992 | tf_op jit(solution)/shard_map/dot_general | solution.py:50
  96.3 8.1 %fusion.148 = f32[1024,512]{0,1:T(8,128)S(1)} fusion(f32[1024,512]{0,1:T(8,128)S(1)} %fusion.149, f32[1024,2048]{1,0:T(8,128)} %get-tuple-element.75, f32[1024]{0:T(1024)S(1)} %get-tuple-element.74, bf16[2048,512]{0,1:T(8,128)(2,1)S(1)} %copy-done.5), kind=kOutput, calls=%fused_computation.141 | convolution fusion | flops 1614807040 | bytes 8916992 | tf_op jit(solution)/shard_map/dot_general | solution.py:50
  108.8 8.1 %fusion.147 = f32[1024,512]{0,1:T(8,128)S(1)} fusion(f32[1024,512]{0,1:T(8,128)S(1)} %fusion.148, f32[1024,2048]{1,0:T(8,128)} %get-tuple-element.77, f32[1024]{0:T(1024)S(1)} %get-tuple-element.76, bf16[2048,512]{0,1:T(8,128)(2,1)S(1)} %copy-done.5), kind=kOutput, calls=%fused_computation.140 | convolution fusion | flops 1614807040 | bytes 8916992 | tf_op jit(solution)/shard_map/dot_general | solution.py:50
  121.2 8.3 %fusion.146 = f32[1024,512]{0,1:T(8,128)S(1)} fusion(f32[1024,512]{0,1:T(8,128)S(1)} %fusion.147, f32[1024,2048]{1,0:T(8,128)} %get-tuple-element.79, f32[1024]{0:T(1024)S(1)} %get-tuple-element.78, bf16[2048,512]{0,1:T(8,128)(2,1)S(1)} %copy-done.5), kind=kOutput, calls=%fused_computation.139 | convolution fusion | flops 1614807040 | bytes 8916992 | tf_op jit(solution)/shard_map/dot_general | solution.py:50
  131.5 5.5 %fusion.145 = f32[1024,512]{0,1:T(8,128)S(1)} fusion(f32[1024,512]{0,1:T(8,128)S(1)} %fusion.146, f32[1024,2048]{1,0:T(8,128)S(1)} %get-tuple-element.81, f32[1024]{0:T(1024)S(1)} %get-tuple-element.80, bf16[2048,512]{0,1:T(8,128)(2,1)S(1)} %copy-done.5), kind=kOutput, calls=%fused_computation.138 | convolution fusion | flops 1614807040 | bytes 8916992 | tf_op jit(solution)/shard_map/dot_general | solution.py:50
  139.3 5.5 %fusion.144 = f32[1024,512]{0,1:T(8,128)S(1)} fusion(f32[1024,512]{0,1:T(8,128)S(1)} %fusion.145, f32[1024,2048]{1,0:T(8,128)S(1)} %get-tuple-element.83, f32[1024]{0:T(1024)S(1)} %get-tuple-element.82, bf16[2048,512]{0,1:T(8,128)(2,1)S(1)} %copy-done.5), kind=kOutput, calls=%fused_computation.137 | convolution fusion | flops 1614807040 | bytes 8916992 | tf_op jit(solution)/shard_map/dot_general | solution.py:50
  146.8 5.5 %fusion.143 = f32[1024,512]{0,1:T(8,128)S(1)} fusion(f32[1024,512]{0,1:T(8,128)S(1)} %fusion.144, f32[1024,2048]{1,0:T(8,128)S(1)} %get-tuple-element.85, f32[1024]{0:T(1024)S(1)} %get-tuple-element.84, bf16[2048,512]{0,1:T(8,128)(2,1)S(1)} %copy-done.5), kind=kOutput, calls=%fused_computation.136 | convolution fusion | flops 1614807040 | bytes 8916992 | tf_op jit(solution)/shard_map/dot_general | solution.py:50
  154.4 5.5 %fusion.142 = f32[1024,512]{0,1:T(8,128)S(1)} fusion(f32[1024,512]{0,1:T(8,128)S(1)} %fusion.143, f32[1024,2048]{1,0:T(8,128)S(1)} %get-tuple-element.87, f32[1024]{0:T(1024)S(1)} %get-tuple-element.86, bf16[2048,512]{0,1:T(8,128)(2,1)S(1)} %copy-done.5), kind=kOutput, calls=%fused_computation.135 | convolution fusion | flops 1614807040 | bytes 8916992 | tf_op jit(solution)/shard_map/dot_general | solution.py:50
  168.8 9.7 %all-to-all-start.1 = ((f32[32,1,256]{2,1,0:T(1,128)}), f32[32,1,256]{2,1,0:T(1,128)}, u32[]{:S(2)}, u32[]{:S(2)}) async-start(f32[32,1,256]{2,1,0:T(1,128)} %reshape.90), calls=%async_computation.1 | async-start | bytes 65536 | tf_op jit(solution)/shard_map/all_to_all | solution.py:128
  237.1 5.9 %all-to-all-start.2 = ((f32[32,1,256]{2,1,0:T(1,128)}), f32[32,1,256]{2,1,0:T(1,128)S(1)}, u32[]{:S(2)}, u32[]{:S(2)}) async-start(f32[32,1,256]{2,1,0:T(1,128)} %reshape.92), calls=%async_computation.2 | async-start | bytes 65536 | tf_op jit(solution)/shard_map/all_to_all | solution.py:127
  243.7 6.6 %all-to-all-done.2 = f32[32,1,256]{2,1,0:T(1,128)S(1)} async-done(((f32[32,1,256]{2,1,0:T(1,128)}), f32[32,1,256]{2,1,0:T(1,128)S(1)}, u32[]{:S(2)}, u32[]{:S(2)}) %all-to-all-start.2) | async-done | bytes 32800 | tf_op jit(solution)/shard_map/all_to_all | solution.py:127
  265.3 37.2 %all-to-all-done = f32[32,1,32,512]{3,2,1,0:T(8,128)} async-done(((f32[32,1,32,512]{3,2,1,0:T(8,128)}), f32[32,1,32,512]{3,2,1,0:T(8,128)}, u32[]{:S(2)}, u32[]{:S(2)}) %all-to-all-start) | async-done | bytes 2097184 | tf_op jit(solution)/shard_map/all_to_all | solution.py:13
  309.3 50.1 %all-gather.2.cloned.1.call-done = bf16[1024,512]{1,0:T(8,128)(2,1)} async-done(((bf16[32,512]{1,0:T(8,128)(2,1)}), bf16[1024,512]{1,0:T(8,128)(2,1)}) %all-gather.2.cloned.1.call-update) | async-done | bytes 1048592 | tf_op jit(solution)/shard_map/all_gather | solution.py:143
  365.3 4.5 multiply_reduce_fusion.3
  369.9 4.5 multiply_reduce_fusion.4
  374.4 4.5 multiply_reduce_fusion.5
  378.9 4.5 multiply_reduce_fusion.6
  383.4 4.7 %multiply_reduce_fusion.7 = (f32[2048]{0:T(1024)S(1)}, f32[2048,1024]{0,1:T(8,128)}) fusion(bf16[1024,512]{0,1:T(8,128)(2,1)S(1)} %convolution_convert_fusion.4, bf16[2048,512]{0,1:T(8,128)(2,1)S(1)} %convolution_convert_fusion.2), kind=kOutput, calls=%fused_computation.26 | convolution fusion | flops 272627712 | bytes 8790016 | tf_op jit(solution)/shard_map/dot_general | solution.py:40
  392.3 4.8 %fusion.25 = f32[2048]{0:T(1024)S(1)} fusion(f32[2048,1024]{0,1:T(8,128)} %get-tuple-element.97, f32[2048]{0:T(1024)S(1)} %get-tuple-element.96), kind=kLoop, calls=%fused_computation.59 | loop fusion | flops 6289408 | bytes 8404992 | tf_op jit(solution)/shard_map/reduce_sum | solution.py:156
  397.1 4.8 %fusion.23 = f32[2048]{0:T(1024)S(1)} fusion(f32[2048,1024]{0,1:T(8,128)} %get-tuple-element.95, f32[2048]{0:T(1024)S(1)} %get-tuple-element.94), kind=kLoop, calls=%fused_computation.57 | loop fusion | flops 6289408 | bytes 8404992 | tf_op jit(solution)/shard_map/reduce_sum | solution.py:156
  401.9 4.8 %fusion.21 = f32[2048]{0:T(1024)S(1)} fusion(f32[2048,1024]{0,1:T(8,128)} %get-tuple-element.93, f32[2048]{0:T(1024)S(1)} %get-tuple-element.92), kind=kLoop, calls=%fused_computation.55 | loop fusion | flops 6289408 | bytes 8404992 | tf_op jit(solution)/shard_map/reduce_sum | solution.py:156
  406.7 4.8 %fusion.19 = f32[2048]{0:T(1024)S(1)} fusion(f32[2048,1024]{0,1:T(8,128)} %get-tuple-element.91, f32[2048]{0:T(1024)S(1)} %get-tuple-element.90), kind=kLoop, calls=%fused_computation.53 | loop fusion | flops 6289408 | bytes 8404992 | tf_op jit(solution)/shard_map/reduce_sum | solution.py:156
  411.5 5.1 %fusion.17 = f32[2048]{0:T(1024)S(1)} fusion(f32[2048,1024]{0,1:T(8,128)} %get-tuple-element.89, f32[2048]{0:T(1024)S(1)} %get-tuple-element.88), kind=kLoop, calls=%fused_computation.51 | loop fusion | flops 6289408 | bytes 8404992 | tf_op jit(solution)/shard_map/reduce_sum | solution.py:156
  417.4 4.9 %fusion.76 = bf16[2048,512]{0,1:T(8,128)(2,1)S(1)} fusion(f32[2048,1024]{0,1:T(8,128)} %get-tuple-element.89, f32[2048]{0:T(1024)S(1)} %get-tuple-element.88, f32[2048]{0:T(1024)S(1)} %fusion.17, bf16[1024,512]{0,1:T(8,128)(2,1)S(1)} %convolution_convert_fusion.3), kind=kOutput, calls=%fused_computation.107 | convolution fusion | flops 274989056 | bytes 8798208 | tf_op jit(solution)/shard_map/dot_general | solution.py:157
  422.3 4.9 %fusion.85 = bf16[2048,512]{0,1:T(8,128)(2,1)S(1)} fusion(bf16[2048,512]{0,1:T(8,128)(2,1)S(1)} %fusion.76, f32[2048,1024]{0,1:T(8,128)} %get-tuple-element.91, f32[2048]{0:T(1024)S(1)} %get-tuple-element.90, f32[2048]{0:T(1024)S(1)} %fusion.19, bf16[1024,512]{0,1:T(8,128)(2,1)S(1)} %convolution_convert_fusion.3), kind=kOutput, calls=%fused_computation.110 | convolution fusion | flops 274989056 | bytes 8798208 | tf_op jit(solution)/shard_map/dot_general | solution.py:157
  427.2 5.1 %fusion.94 = bf16[2048,512]{0,1:T(8,128)(2,1)S(1)} fusion(bf16[2048,512]{0,1:T(8,128)(2,1)S(1)} %fusion.85, f32[2048,1024]{0,1:T(8,128)} %get-tuple-element.93, f32[2048]{0:T(1024)S(1)} %get-tuple-element.92, f32[2048]{0:T(1024)S(1)} %fusion.21, bf16[1024,512]{0,1:T(8,128)(2,1)S(1)} %convolution_convert_fusion.3), kind=kOutput, calls=%fused_computation.113 | convolution fusion | flops 274989056 | bytes 8798208 | tf_op jit(solution)/shard_map/dot_general | solution.py:157
  432.3 5.1 %fusion.103 = bf16[2048,512]{0,1:T(8,128)(2,1)S(1)} fusion(bf16[2048,512]{0,1:T(8,128)(2,1)S(1)} %fusion.94, f32[2048,1024]{0,1:T(8,128)} %get-tuple-element.95, f32[2048]{0:T(1024)S(1)} %get-tuple-element.94, f32[2048]{0:T(1024)S(1)} %fusion.23, bf16[1024,512]{0,1:T(8,128)(2,1)S(1)} %convolution_convert_fusion.3), kind=kOutput, calls=%fused_computation.116 | convolution fusion | flops 274989056 | bytes 8798208 | tf_op jit(solution)/shard_map/dot_general | solution.py:157
  (179 shorter events, 169.8 us)
Async XLA Ops:
  6.5 45.5 %copy-start = (bf16[512,512]{1,0:T(8,128)(2,1)S(1)}, bf16[512,512]{1,0:T(8,128)(2,1)}, u32[]{:S(2)}) copy-start(bf16[512,512]{1,0:T(8,128)(2,1)} %param.17) | copy-start | bytes 1572868
  6.5 9.2 %copy-start.10 = (f32[27,512]{1,0:T(8,128)S(1)}, f32[27,512]{1,0:T(8,128)}, u32[]{:S(2)}) copy-start(f32[27,512]{1,0:T(8,128)} %param.14) | copy-start | bytes 165892
  6.5 9.2 %copy-start.11 = (bf16[1024,512]{1,0:T(8,128)(2,1)S(1)}, bf16[1024,512]{1,0:T(8,128)(2,1)}, u32[]{:S(2)}) copy-start(bf16[1024,512]{1,0:T(8,128)(2,1)} %param.15) | copy-start | bytes 3145732
  6.5 9.2 %copy-start.13 = (bf16[512,512]{1,0:T(8,128)(2,1)S(1)}, bf16[512,512]{1,0:T(8,128)(2,1)}, u32[]{:S(2)}) copy-start(bf16[512,512]{1,0:T(8,128)(2,1)} %param.16) | copy-start | bytes 1572868
  9.5 26.2 %copy-start.2 = (bf16[8,16,16,512]{3,2,1,0:T(8,128)(2,1)}, bf16[8,16,16,512]{3,2,1,0:T(8,128)(2,1)S(1)}, u32[]{:S(2)}) copy-start(bf16[8,16,16,512]{3,2,1,0:T(8,128)(2,1)S(1)} %broadcast_multiply_fusion) | copy-start | bytes 6291460
  9.5 16.0 %collective-permute-start = (bf16[1,16,16,512]{3,2,1,0:T(8,128)(2,1)S(1)}, bf16[1,16,16,512]{3,2,1,0:T(8,128)(2,1)S(1)}, u32[]{:S(2)}, u32[]{:S(2)}) collective-permute-start(bf16[1,16,16,512]{3,2,1,0:T(8,128)(2,1)S(1)} %get-tuple-element.43), channel_id=1, source_target_pairs={{0,4},{4,8},{8,12},{12,16},{16,20},{20,24},{24,28},{1,5},{5,9},{9,... | collective-permute-start | bytes 786440 | tf_op jit(solution)/shard_map/ppermute | solution.py:25
  14.4 11.2 %collective-permute-start.1 = (bf16[1,16,16,512]{3,2,1,0:T(8,128)(2,1)S(1)}, bf16[1,16,16,512]{3,2,1,0:T(8,128)(2,1)S(1)}, u32[]{:S(2)}, u32[]{:S(2)}) collective-permute-start(bf16[1,16,16,512]{3,2,1,0:T(8,128)(2,1)S(1)} %get-tuple-element.44), channel_id=1, source_target_pairs={{4,0},{8,4},{12,8},{16,12},{20,16},{24,20},{28,24},{5,1},{9,5},{13... | collective-permute-start | bytes 786440 | tf_op jit(solution)/shard_map/ppermute | solution.py:27
  25.6 2.6 collective-permute-start.2
  26.9 5.0 %collective-permute-start.3 = (bf16[10,1,16,512]{3,2,1,0:T(8,128)(2,1)S(1)}, bf16[10,1,16,512]{3,2,1,0:T(8,128)(2,1)S(1)}, u32[]{:S(2)}, u32[]{:S(2)}) collective-permute-start(bf16[10,1,16,512]{3,2,1,0:T(8,128)(2,1)S(1)} %get-tuple-element.10), channel_id=1, source_target_pairs={{1,0},{2,1},{3,2},{5,4},{6,5},{7,6},{9,8},{10,9},{11,10},{13,12},{... | collective-permute-start | bytes 491528 | tf_op jit(solution)/shard_map/ppermute | solution.py:27
  52.1 24.7 %copy-start.4 = (bf16[8,16,16,512]{3,2,1,0:T(8,128)(2,1)}, bf16[8,16,16,512]{3,2,1,0:T(8,128)(2,1)S(1)}, u32[]{:S(2)}) copy-start(bf16[8,16,16,512]{3,2,1,0:T(8,128)(2,1)S(1)} %add_convert_fusion) | copy-start | bytes 6291460
  72.3 4.5 copy-start.14
  79.6 4.5 copy-start.5
  168.8 68.3 %all-to-all-start.1 = ((f32[32,1,256]{2,1,0:T(1,128)}), f32[32,1,256]{2,1,0:T(1,128)}, u32[]{:S(2)}, u32[]{:S(2)}) async-start(f32[32,1,256]{2,1,0:T(1,128)} %reshape.90), calls=%async_computation.1 | async-start | bytes 65536 | tf_op jit(solution)/shard_map/all_to_all | solution.py:128
  180.9 29.8 %copy-start.7 = (f32[1,1,32,512]{2,3,1,0:T(8,128)S(1)}, f32[1,1,32,512]{2,3,1,0:T(8,128)}, u32[]{:S(2)}) copy-start(f32[1,1,32,512]{2,3,1,0:T(8,128)} %get-tuple-element.20) | copy-start | bytes 196612
  180.9 29.9 %copy-start.6 = (f32[1,1,32,512]{2,3,1,0:T(8,128)S(1)}, f32[1,1,32,512]{2,3,1,0:T(8,128)}, u32[]{:S(2)}) copy-start(f32[1,1,32,512]{2,3,1,0:T(8,128)} %get-tuple-element.21) | copy-start | bytes 196612
  237.1 13.2 %all-to-all-start.2 = ((f32[32,1,256]{2,1,0:T(1,128)}), f32[32,1,256]{2,1,0:T(1,128)S(1)}, u32[]{:S(2)}, u32[]{:S(2)}) async-start(f32[32,1,256]{2,1,0:T(1,128)} %reshape.92), calls=%async_computation.2 | async-start | bytes 65536 | tf_op jit(solution)/shard_map/all_to_all | solution.py:127
  250.3 52.2 %all-to-all-start = ((f32[32,1,32,512]{3,2,1,0:T(8,128)}), f32[32,1,32,512]{3,2,1,0:T(8,128)}, u32[]{:S(2)}, u32[]{:S(2)}) async-start(f32[32,1,32,512]{3,2,1,0:T(8,128)} %constant_dynamic-update-slice_fusion), calls=%async_computation | async-start | bytes 4194304 | tf_op jit(solution)/shard_map/all_to_all | solution.py:13
  253.8 105.6 %all-gather.2.cloned.1.call-start = ((), (), s32[]{:S(2)}) async-start(), calls=%async_computation.3 | async-start | bytes 1081344 | tf_op jit(solution)/shard_map/all_gather | solution.py:143
  261.4 43.2 %copy-start.9 = (bf16[512,512]{1,0:T(8,128)(2,1)S(1)}, bf16[512,512]{1,0:T(8,128)(2,1)}, u32[]{:S(2)}) copy-start(bf16[512,512]{1,0:T(8,128)(2,1)} %param.19) | copy-start | bytes 1572868
  306.2 53.2 %copy-start.15 = (bf16[512,512]{1,0:T(8,128)(2,1)S(1)}, bf16[512,512]{1,0:T(8,128)(2,1)}, u32[]{:S(2)}) copy-start(bf16[512,512]{1,0:T(8,128)(2,1)} %param.21) | copy-start | bytes 1572868
  411.5 5.1 %copy-start.12 = (bf16[1024,512]{1,0:T(8,128)(2,1)S(1)}, bf16[1024,512]{1,0:T(8,128)(2,1)}, u32[]{:S(2)}) copy-start(bf16[1024,512]{1,0:T(8,128)(2,1)} %all-gather.2.cloned.1.call-done) | copy-start | bytes 3145732
  411.5 5.1 %copy-start.16 = (bf16[512,512]{1,0:T(8,128)(2,1)S(1)}, bf16[512,512]{1,0:T(8,128)(2,1)}, u32[]{:S(2)}) copy-start(bf16[512,512]{1,0:T(8,128)(2,1)} %param.22) | copy-start | bytes 1572868
  427.2 10.2 %slice-start = ((s8[8388608]{0:T(1024)(128)(4,1)}), s8[4194304]{0:T(1024)(128)(4,1)S(1)}, s32[]{:S(2)}) async-start(s8[8388608]{0:T(1024)(128)(4,1)} %bitcast.142), calls=%async_computation.4 | async-start | bytes 8388608
  432.3 5.1 %slice-start.1 = ((s8[8388608]{0:T(1024)(128)(4,1)}), s8[4194304]{0:T(1024)(128)(4,1)S(1)}, s32[]{:S(2)}) async-start(s8[8388608]{0:T(1024)(128)(4,1)} %bitcast.142), calls=%async_computation.5 | async-start | bytes 8388608
  442.1 1.6 copy-start.3
  442.1 1.7 copy-start.8
  442.1 5.0 %copy-start.1 = (bf16[512,512]{1,0:T(8,128)(2,1)S(1)}, bf16[512,512]{1,0:T(8,128)(2,1)}, u32[]{:S(2)}) copy-start(bf16[512,512]{1,0:T(8,128)(2,1)} %param.17) | copy-start | bytes 1572868
Sparse Core Ops, SparseCore 0:
  306.4 53.0 all-gather.1
